TPU v7x, 256 devices: a whole 4x4x8 slice. The times are simulated.
256 devices in a mesh: fsdp: 64 (over y, z, core), tensor: 4 (over x).
Axes of the slice: x: 4, y: 4, z: 8, core: 2. Of those that a mesh axis runs over, the one named last changes fastest.
Arguments:
- layer_input: bfloat16 [16384, 8192], P('fsdp', 'tensor'), may hold values from -6 to 6
- value_grad: bfloat16 [16384, 1024], P('fsdp', 'tensor'), may hold values from -6 to 6
- quant_codes: int32 [8192, 1024], P('fsdp', 'tensor'), may hold values from 0 to 15
- block_scales: float32 [8192, 16], P('fsdp', 'tensor'), may hold values from 0.02 to 0.08
- tenant_ids: int32 [1024], P('fsdp'), may hold values from 0 to 63
- live_counts: int32 [64], P('fsdp'), may hold values from 12 to 16, as said below
- tenant_owner: int32 [64], replicated, may hold values from 0 to 63, each once
- factor_down: float32 [64, 16, 8192], P('fsdp', None, 'tensor'), may hold values from -6 to 6
- factor_up: float32 [64, 16, 1024], P('fsdp', None, 'tensor'), may hold values from -6 to 6
- moment_down: float32 [64, 16, 8192], P('fsdp', None, 'tensor'), may hold values from -6 to 6
- second_down: float32 [64, 16, 8192], P('fsdp', None, 'tensor'), may hold values from 0.05 to 5
- moment_up: float32 [64, 16, 1024], P('fsdp', None, 'tensor'), may hold values from -6 to 6
- second_up: float32 [64, 16, 1024], P('fsdp', None, 'tensor'), may hold values from 0.05 to 5
Outputs:
- layer_input_gradient: bfloat16 [16384, 8192], P('fsdp', 'tensor')
- new_down: float32 [64, 16, 8192], P('fsdp', None, 'tensor')
- new_up: float32 [64, 16, 1024], P('fsdp', None, 'tensor')
- new_moment_down: float32 [64, 16, 8192], P('fsdp', None, 'tensor')
- new_second_down: float32 [64, 16, 8192], P('fsdp', None, 'tensor')
- new_moment_up: float32 [64, 16, 1024], P('fsdp', None, 'tensor')
- new_second_up: float32 [64, 16, 1024], P('fsdp', None, 'tensor')
Inputs may be any that keep to these rules, and one draw needn't show every extreme that they name: The first live_counts[f] sequence slots of fsdp index f are live and the rest are padding; some index has all 16 live. tenant_owner is a permutation: tenant t's adapter and its moments sit in slot tenant_owner[t].
All inputs are finite; a program needn't handle non-finite values.
Results may differ from a plain program's by a relative error of at most 0.01.
Values may be sent and summed in bfloat16 or wider, within the bound.
No kernel may reach another device: no remote copies, remote signals or barrier semaphores. Data moves between devices by JAX's collectives and lax.ppermute only.
A program may use at most 128 MiB of HBM per device.

v0:
```python
import math
import jax
import jax.numpy as jnp
from jax import lax
from jax.sharding import PartitionSpec as P

MODEL_WIDTH = 8192
ADAPTER_RANK = 16
nf4_levels = (
    -1.0,
    -0.6962,
    -0.5251,
    -0.3949,
    -0.2844,
    -0.1848,
    -0.0911,
    0.0,
    0.0796,
    0.1609,
    0.2461,
    0.3379,
    0.4407,
    0.5626,
    0.723,
    1.0,
)
adapter_scale = 2.0
beta_one = 0.9
beta_two = 0.999
adam_step = 10.0
learn_rate = 0.05
decay_rate = 0.01
adam_eps = 1e-08


def sent_together(arrays, axis, dim, along):
    ends, at = ([], 0)
    for a in arrays[:-1]:
        at += a.shape[along]
        ends.append(at)
    both = jnp.concatenate(arrays, axis=along)
    return tuple(jnp.split(lax.all_gather(both, axis, axis=dim, tiled=True), ends, axis=along))


def sent_to_all(x, axis):
    length = lax.axis_size(axis)
    return lax.all_to_all(jnp.broadcast_to(x[None], (length, *x.shape)), axis, 0, 0, tiled=True)


def over_copies(x, axis):
    return sent_to_all(x, axis).sum(axis=0)


def packed_total(arrays, axis):
    ends = [0]
    for a in arrays:
        ends.append(ends[-1] + a.size)
    total = over_copies(jnp.concatenate([a.ravel() for a in arrays]), axis)
    return tuple((total[b:e].reshape(a.shape) for a, b, e in zip(arrays, ends, ends[1:])))


def adam_update(param, grad, moment, second):
    new_moment = beta_one * moment + (1.0 - beta_one) * grad
    new_second = beta_two * second + (1.0 - beta_two) * grad * grad
    corrected = new_moment / (1.0 - beta_one**adam_step)
    divisor = jnp.sqrt(new_second / (1.0 - beta_two**adam_step)) + adam_eps
    new_param = param - learn_rate * (corrected / divisor + decay_rate * param)
    return (new_param, new_moment, new_second)


def dequantize(quant_codes, block_scales):
    levels_out = jnp.zeros(quant_codes.shape, jnp.float32)
    for position in range(16):
        levels_out = jnp.where(quant_codes == position, nf4_levels[position], levels_out)
    row_count, col_count = quant_codes.shape
    blocks = block_scales.shape[1]
    scaled = levels_out.reshape(row_count, blocks, col_count // blocks) * block_scales[:, :, None]
    return scaled.reshape(row_count, col_count).astype(jnp.bfloat16)


def right_product(left, right):
    return lax.dot_general(
        left, right, (((1,), (1,)), ((), ())), preferred_element_type=jnp.float32
    )


def left_product(left, right):
    return lax.dot_general(
        left, right, (((0,), (0,)), ((), ())), preferred_element_type=jnp.float32
    )


def add_sources(pieces):
    return (jnp.sum(pieces[0], axis=0, keepdims=True), jnp.sum(pieces[1], axis=0, keepdims=True))


def shards(
    layer_input,
    value_grad,
    quant_codes,
    block_scales,
    tenant_ids,
    live_counts,
    tenant_owner,
    factor_down,
    factor_up,
    moment_down,
    second_down,
    moment_up,
    second_up,
):
    tok_rows, width_part = layer_input.shape
    value_part = value_grad.shape[1]
    slot_count = tenant_ids.shape[0]
    seq_len = tok_rows // slot_count
    tenant_total = tenant_owner.shape[0]
    rank_size = factor_down.shape[1]
    inverse_width = 1.0 / math.sqrt(MODEL_WIDTH)
    coefficient = adapter_scale / math.sqrt(ADAPTER_RANK)
    live_seq = jnp.arange(slot_count, dtype=jnp.int32) < live_counts[0]
    live_tok = jnp.broadcast_to(live_seq[:, None], (slot_count, seq_len)).reshape(tok_rows)
    masked = jnp.where(live_tok[:, None], value_grad, jnp.zeros_like(value_grad))
    tenant_iota = jnp.arange(tenant_total, dtype=jnp.int32)
    matches = tenant_ids[:, None] == tenant_iota[None, :]
    slot_seq = jnp.sum(jnp.where(matches, tenant_owner[None, :], 0), axis=1)
    onehot_seq = (slot_seq[:, None] == tenant_iota[None, :]).astype(jnp.bfloat16)
    weight_local = dequantize(quant_codes, block_scales)
    all_down, all_up = sent_together(
        (factor_down.astype(jnp.bfloat16), factor_up.astype(jnp.bfloat16)), "fsdp", 0, 2
    )
    partial_value = right_product(masked, lax.all_gather(weight_local, "fsdp", axis=0, tiled=True))
    base_input_grad = lax.psum_scatter(
        partial_value.astype(jnp.bfloat16), "tensor", scatter_dimension=1, tiled=True
    ).astype(jnp.float32)
    flattened_down = all_down.reshape(tenant_total * rank_size, width_part)
    up_flat = all_up.reshape(tenant_total * rank_size, value_part)
    onehot_tok = jnp.broadcast_to(
        onehot_seq[:, None, :], (slot_count, seq_len, tenant_total)
    ).reshape(tok_rows, tenant_total)
    selector = onehot_tok.astype(jnp.float32)[:, :, None]
    down_scores = right_product(layer_input, flattened_down).reshape(
        tok_rows, tenant_total, rank_size
    )
    up_scores = right_product(masked, up_flat).reshape(tok_rows, tenant_total, rank_size)
    in_part = jnp.sum(down_scores * selector, axis=1) * inverse_width
    grad_part = jnp.sum(up_scores * selector, axis=1) * coefficient
    in_sum, grad_sum = packed_total((in_part, grad_part), "tensor")
    input_lowrank = in_sum.astype(jnp.bfloat16)
    gradient_lowrank = grad_sum.astype(jnp.bfloat16)
    spread_gradient = (onehot_tok[:, :, None] * gradient_lowrank[:, None, :]).reshape(
        tok_rows, tenant_total * rank_size
    )
    in_spread = (onehot_tok[:, :, None] * input_lowrank[:, None, :]).reshape(
        tok_rows, tenant_total * rank_size
    )
    adapter_input_grad = (
        jnp.dot(spread_gradient, flattened_down, preferred_element_type=jnp.float32) * inverse_width
    )
    down_terms = (left_product(spread_gradient, layer_input) * inverse_width).reshape(
        tenant_total, rank_size, width_part
    )
    up_terms = (left_product(in_spread, masked) * coefficient).reshape(
        tenant_total, rank_size, value_part
    )
    down_gradient, up_gradient = add_sources(
        (
            lax.all_to_all(
                down_terms.astype(jnp.bfloat16), "fsdp", split_axis=0, concat_axis=0, tiled=True
            ).astype(down_terms.dtype),
            lax.all_to_all(
                up_terms.astype(jnp.bfloat16), "fsdp", split_axis=0, concat_axis=0, tiled=True
            ).astype(up_terms.dtype),
        )
    )
    layer_input_gradient = (base_input_grad + adapter_input_grad).astype(jnp.bfloat16)
    new_down, new_moment_down, new_second_down = adam_update(
        factor_down, down_gradient, moment_down, second_down
    )
    new_up, new_moment_up, new_second_up = adam_update(factor_up, up_gradient, moment_up, second_up)
    return (
        layer_input_gradient,
        new_down,
        new_up,
        new_moment_down,
        new_second_down,
        new_moment_up,
        new_second_up,
    )


def solution(mesh):
    in_specs = (
        P("fsdp", "tensor"),
        P("fsdp", "tensor"),
        P("fsdp", "tensor"),
        P("fsdp", "tensor"),
        P("fsdp"),
        P("fsdp"),
        P(),
        P("fsdp", None, "tensor"),
        P("fsdp", None, "tensor"),
        P("fsdp", None, "tensor"),
        P("fsdp", None, "tensor"),
        P("fsdp", None, "tensor"),
        P("fsdp", None, "tensor"),
    )
    out_specs = (
        P("fsdp", "tensor"),
        P("fsdp", None, "tensor"),
        P("fsdp", None, "tensor"),
        P("fsdp", None, "tensor"),
        P("fsdp", None, "tensor"),
        P("fsdp", None, "tensor"),
        P("fsdp", None, "tensor"),
    )
    return jax.shard_map(shards, mesh=mesh, in_specs=in_specs, out_specs=out_specs, check_vma=False)
```

profile of v0, /device:TPU:1, one launch (start us, length us, event | category | flops | bytes accessed | tf_op | source)
XLA Modules:
  0.0 329.7 jit_solution(11363798175707540958)
XLA Ops:
  7.2 1.1 copy.97
  8.3 1.5 fusion.10
  9.9 0.7 convert_element_type.63
  10.6 0.9 convert_element_type.62
  11.5 0.6 pad_maximum_fusion
  13.0 0.9 select_reduce_fusion
  14.1 77.3 %all-gather.3.cloned.1.call-done = bf16[8192,256]{0,1:T(8,128)(2,1)} async-done(((bf16[128,256]{0,1:T(8,128)(2,1)}), bf16[8192,256]{0,1:T(8,128)(2,1)}) %all-gather.3.cloned.1.call-update) | async-done | bytes 4194320 | tf_op jit(solution)/shard_map/all_gather | solution.py:131
  91.3 5.6 %convolution_convert_fusion = bf16[256,8192]{1,0:T(8,128)(2,1)} fusion(bf16[8192,256]{0,1:T(8,128)(2,1)} %all-gather.3.cloned.1.call-done, bf16[256,256]{1,0:T(8,128)(2,1)} %param.14, pred[256]{0:T(512)(128)(4,1)S(1)} %broadcast_in_dim.105), kind=kOutput, calls=%fused_computation | convolution fusion | flops 1075904512 | bytes 8519936 | tf_op jit(solution)/shard_map/dot_general | solution.py:82
  97.0 76.3 %all-gather.5.cloned.1.call-done = bf16[64,16,2304]{2,1,0:T(8,128)(2,1)} async-done(((bf16[1,16,2304]{2,1,0:T(8,128)(2,1)}), bf16[64,16,2304]{2,1,0:T(8,128)(2,1)}) %all-gather.5.cloned.1.call-update) | async-done | bytes 4718608 | tf_op jit(solution)/shard_map/all_gather | solution.py:42
  173.3 1.1 split.9
  174.8 2.2 slice-done
  177.0 1.3 fusion.20
  179.3 0.7 broadcast_in_dim.127
  180.1 4.1 %all-to-all-start = ((f32[4,1,8192]{2,1,0:T(1,128)}), f32[4,1,8192]{2,1,0:T(1,128)S(1)}, u32[]{:S(2)}, u32[]{:S(2)}) async-start(f32[4,1,8192]{2,1,0:T(1,128)} %broadcast_in_dim.127), calls=%async_computation.1 | async-start | bytes 262144 | tf_op jit(solution)/shard_map/all_to_all | solution.py:47
  184.2 6.3 %all-to-all-done = f32[4,1,8192]{2,1,0:T(1,128)S(1)} async-done(((f32[4,1,8192]{2,1,0:T(1,128)}), f32[4,1,8192]{2,1,0:T(1,128)S(1)}, u32[]{:S(2)}, u32[]{:S(2)}) %all-to-all-start) | async-done | bytes 131104 | tf_op jit(solution)/shard_map/all_to_all | solution.py:47
  191.1 1.2 fusion.3
  192.3 7.4 %all-to-all-start.2 = ((bf16[64,16,256]{2,1,0:T(8,128)(2,1)}), bf16[64,16,256]{2,1,0:T(8,128)(2,1)S(1)}, u32[]{:S(2)}, u32[]{:S(2)}) async-start(bf16[64,16,256]{2,1,0:T(8,128)(2,1)} %bitcast.12), calls=%async_computation.3 | async-start | bytes 1048576 | tf_op jit(solution)/shard_map/all_to_all | solution.py:170
  199.7 3.2 multiply_convert_fusion
  202.9 14.1 %all-to-all-done.2 = bf16[64,16,256]{2,1,0:T(8,128)(2,1)S(1)} async-done(((bf16[64,16,256]{2,1,0:T(8,128)(2,1)}), bf16[64,16,256]{2,1,0:T(8,128)(2,1)S(1)}, u32[]{:S(2)}, u32[]{:S(2)}) %all-to-all-start.2) | async-done | bytes 524320 | tf_op jit(solution)/shard_map/all_to_all | solution.py:170
  217.0 6.6 %all-to-all-start.1 = ((bf16[64,16,2048]{2,1,0:T(8,128)(2,1)}), bf16[64,16,2048]{2,1,0:T(8,128)(2,1)}, u32[]{:S(2)}, u32[]{:S(2)}) async-start(bf16[64,16,2048]{2,1,0:T(8,128)(2,1)} %bitcast.48), calls=%async_computation.2 | async-start | bytes 8388608 | tf_op jit(solution)/shard_map/all_to_all | solution.py:167
  224.4 4.7 %fusion.2 = bf16[256,2048]{1,0:T(8,128)(2,1)} fusion(bf16[256,2048]{1,0:T(8,128)(2,1)} %reduce-scatter.2.cloned.1.call-done, bf16[256,16]{0,1:T(8,128)(2,1)S(1)} %copy.120, bf16[256,64]{0,1:T(8,128)(2,1)S(1)} %copy.113, bf16[64,16,2304]{2,1,0:T(8,128)(2,1)} %all-gather.5.cloned.1.call-done), kind=kOutput, calls=%fused_computation.6 | convolution fusion | flops 1076101120 | bytes 6332416 | tf_op jit(solution)/shard_map/dot_general | solution.py:157
  229.1 90.3 %all-to-all-done.1 = bf16[64,16,2048]{2,1,0:T(8,128)(2,1)} async-done(((bf16[64,16,2048]{2,1,0:T(8,128)(2,1)}), bf16[64,16,2048]{2,1,0:T(8,128)(2,1)}, u32[]{:S(2)}, u32[]{:S(2)}) %all-to-all-start.1) | async-done | bytes 4194336 | tf_op jit(solution)/shard_map/all_to_all | solution.py:167
  319.5 2.9 convert_reduce_fusion
  322.4 0.8 multiply_subtract_fusion
  (50 shorter events, 3.4 us)
Async XLA Ops:
  7.2 167.7 %copy-start = (bf16[256,2048]{1,0:T(8,128)(2,1)S(1)}, bf16[256,2048]{1,0:T(8,128)(2,1)}, u32[]{:S(2)}) copy-start(bf16[256,2048]{1,0:T(8,128)(2,1)} %param.13) | copy-start | bytes 3145732
  7.2 84.2 %all-gather.3.cloned.1.call-start = ((), (), s32[]{:S(2)}) async-start(), calls=%async_computation.4 | async-start | bytes 4259840 | tf_op jit(solution)/shard_map/all_gather | solution.py:131
  9.8 163.5 %all-gather.5.cloned.1.call-start = ((), (), s32[]{:S(2)}) async-start(), calls=%async_computation.6 | async-start | bytes 4792320 | tf_op jit(solution)/shard_map/all_gather | solution.py:42
  12.1 212.2 %reduce-scatter.2.cloned.1.call-start = ((), (), s32[]{:S(2)}) async-start(), calls=%async_computation.5 | async-start | bytes 5242880 | tf_op jit(solution)/shard_map/reduce_scatter | solution.py:132
  96.9 77.4 %copy-start.2 = (bf16[256,256]{1,0:T(8,128)(2,1)S(1)}, bf16[256,256]{1,0:T(8,128)(2,1)}, u32[]{:S(2)}) copy-start(bf16[256,256]{1,0:T(8,128)(2,1)} %param.14) | copy-start | bytes 393220
  174.8 2.2 slice-start
  180.1 10.4 %all-to-all-start = ((f32[4,1,8192]{2,1,0:T(1,128)}), f32[4,1,8192]{2,1,0:T(1,128)S(1)}, u32[]{:S(2)}, u32[]{:S(2)}) async-start(f32[4,1,8192]{2,1,0:T(1,128)} %broadcast_in_dim.127), calls=%async_computation.1 | async-start | bytes 262144 | tf_op jit(solution)/shard_map/all_to_all | solution.py:47
  192.3 24.7 %all-to-all-start.2 = ((bf16[64,16,256]{2,1,0:T(8,128)(2,1)}), bf16[64,16,256]{2,1,0:T(8,128)(2,1)S(1)}, u32[]{:S(2)}, u32[]{:S(2)}) async-start(bf16[64,16,256]{2,1,0:T(8,128)(2,1)} %bitcast.12), calls=%async_computation.3 | async-start | bytes 1048576 | tf_op jit(solution)/shard_map/all_to_all | solution.py:170
  217.0 6.7 %copy-start.5 = (f32[1,16,256]{2,1,0:T(8,128)S(1)}, f32[1,16,256]{2,1,0:T(8,128)}, u32[]{:S(2)}) copy-start(f32[1,16,256]{2,1,0:T(8,128)} %param.21) | copy-start | bytes 49156
  217.0 6.7 %copy-start.6 = (f32[1,16,256]{2,1,0:T(8,128)S(1)}, f32[1,16,256]{2,1,0:T(8,128)}, u32[]{:S(2)}) copy-start(f32[1,16,256]{2,1,0:T(8,128)} %param.24) | copy-start | bytes 49156
  217.0 6.7 %copy-start.7 = (f32[1,16,256]{2,1,0:T(8,128)S(1)}, f32[1,16,256]{2,1,0:T(8,128)}, u32[]{:S(2)}) copy-start(f32[1,16,256]{2,1,0:T(8,128)} %param.25) | copy-start | bytes 49156
  217.0 102.5 %all-to-all-start.1 = ((bf16[64,16,2048]{2,1,0:T(8,128)(2,1)}), bf16[64,16,2048]{2,1,0:T(8,128)(2,1)}, u32[]{:S(2)}, u32[]{:S(2)}) async-start(bf16[64,16,2048]{2,1,0:T(8,128)(2,1)} %bitcast.48), calls=%async_computation.2 | async-start | bytes 8388608 | tf_op jit(solution)/shard_map/all_to_all | solution.py:167
  229.1 93.2 %copy-start.1 = (f32[1,16,2048]{2,1,0:T(8,128)S(1)}, f32[1,16,2048]{2,1,0:T(8,128)}, u32[]{:S(2)}) copy-start(f32[1,16,2048]{2,1,0:T(8,128)} %param.20) | copy-start | bytes 393220
  229.1 93.2 %copy-start.3 = (f32[1,16,2048]{2,1,0:T(8,128)S(1)}, f32[1,16,2048]{2,1,0:T(8,128)}, u32[]{:S(2)}) copy-start(f32[1,16,2048]{2,1,0:T(8,128)} %param.22) | copy-start | bytes 393220
  229.1 93.2 %copy-start.4 = (f32[1,16,2048]{2,1,0:T(8,128)S(1)}, f32[1,16,2048]{2,1,0:T(8,128)}, u32[]{:S(2)}) copy-start(f32[1,16,2048]{2,1,0:T(8,128)} %param.23) | copy-start | bytes 393220
Sparse Core Ops, SparseCore 0:
  11.1 80.1 all-gather.2
  94.7 78.5 all-gather.4
  175.8 47.7 reduce-scatter.1
where the time goes:
time: 330 us
  waiting for transfers between devices  264 us (80%)
  starting transfers between devices  18.2 us (6%)
  matrix products  16.4 us (5%)
  between operations  14.6 us (4%)
  other arithmetic  9.92 us (3%)
  local copies, waits for them, and re-layouts  6.16 us (2%)
    all_to_all x1, waiting for transfers between devices, shards(): lax.all_to_all(down_terms.astype(jnp.bfloat16), 'fsdp', split_axis=0, con...  90.3 us
    all_gather x1, waiting for transfers between devices, shards(): lax.all_gather(weight_local, 'fsdp', axis=0, tiled=True)  77.3 us
    all_gather x1, waiting for transfers between devices, sent_together(): lax.all_gather(both, axis, axis=dim, tiled=True)  76.3 us
    all_to_all x1, waiting for transfers between devices, shards(): lax.all_to_all(up_terms.astype(jnp.bfloat16), 'fsdp', split_axis=0, conca...  14.1 us
    all_to_all x1, starting transfers between devices, shards(): lax.all_to_all(up_terms.astype(jnp.bfloat16), 'fsdp', split_axis=0, conca...  7.43 us
    dot_general x3, matrix products, right_product(): lax.dot_general(left, right, (((1,), (1,)), ((), ())), preferred_element_...  7.3 us
    all_to_all x1, starting transfers between devices, shards(): lax.all_to_all(down_terms.astype(jnp.bfloat16), 'fsdp', split_axis=0, con...  6.61 us
  transfers between devices with their start and end apart: 6, of which 5 were waited for; matrix products, arithmetic and copies ran while one was open for 7% of the time, Pallas kernels for 0%

commit v1 on v0

--- a/solution.py
+++ b/solution.py
@@ -128,7 +128,12 @@
     all_down, all_up = sent_together(
         (factor_down.astype(jnp.bfloat16), factor_up.astype(jnp.bfloat16)), "fsdp", 0, 2
     )
-    partial_value = right_product(masked, lax.all_gather(weight_local, "fsdp", axis=0, tiled=True))
+    partial_value = right_product(
+        masked,
+        jnp.concatenate(
+            lax.all_to_all(jnp.stack([weight_local] * lax.axis_size("fsdp")), "fsdp", 0, 0), axis=0
+        ),
+    )
     base_input_grad = lax.psum_scatter(
         partial_value.astype(jnp.bfloat16), "tensor", scatter_dimension=1, tiled=True
     ).astype(jnp.float32)

time: 330 us -> 301 us (0.912)
  waiting for transfers between devices: 264 us -> 220 us
  starting transfers between devices: 18.2 us -> 30.3 us
    all_to_all x0 -> x1, waiting for transfers between devices: none -> 108 us  [shards(): lax.all_to_all(jnp.stack([weight_local] * lax.axis_size('fsdp')), 'fsdp',...]
    all_gather x1 -> x0, waiting for transfers between devices: 77.3 us -> none  [shards(): lax.all_gather(weight_local, 'fsdp', axis=0, tiled=True)]
    all_gather x1, waiting for transfers between devices: 76.3 us -> 0.02 us  [sent_together(): lax.all_gather(both, axis, axis=dim, tiled=True)]
    all_to_all x0 -> x1, starting transfers between devices: none -> 13.5 us  [shards(): lax.all_to_all(jnp.stack([weight_local] * lax.axis_size('fsdp')), 'fsdp',...]
  transfers between devices with their start and end apart: 6 -> 6, of which waited for: 5 -> 4; matrix products, arithmetic and copies ran while one was open for 7% -> 8% of each run, Pallas kernels for 0% -> 0%
where the time goes in v1:
time: 301 us; the launch traced here: 300 us
  waiting for transfers between devices  220 us (73%)
  starting transfers between devices  30.3 us (10%)
  between operations  16.4 us (5%)
  matrix products  16.3 us (5%)
  local copies, waits for them, and re-layouts  8.72 us (3%)
  other arithmetic  8.69 us (3%)
    all_to_all x1, waiting for transfers between devices, shards(): lax.all_to_all(jnp.stack([weight_local] * lax.axis_size('fsdp')), 'fsdp',...  108 us
    all_to_all x1, waiting for transfers between devices, shards(): lax.all_to_all(down_terms.astype(jnp.bfloat16), 'fsdp', split_axis=0, con...  90.3 us
    all_to_all x1, waiting for transfers between devices, shards(): lax.all_to_all(up_terms.astype(jnp.bfloat16), 'fsdp', split_axis=0, conca...  14.1 us
    all_to_all x1, starting transfers between devices, shards(): lax.all_to_all(jnp.stack([weight_local] * lax.axis_size('fsdp')), 'fsdp',...  13.5 us
    dot_general x3, matrix products, right_product(): lax.dot_general(left, right, (((1,), (1,)), ((), ())), preferred_element_...  7.22 us
    all_to_all x1, waiting for transfers between devices, sent_to_all(): lax.all_to_all(jnp.broadcast_to(x[None], (length, *x.shape)), axis, 0, 0,...  6.96 us
    all_to_all x1, starting transfers between devices, shards(): lax.all_to_all(down_terms.astype(jnp.bfloat16), 'fsdp', split_axis=0, con...  6.61 us
    all_to_all x1, starting transfers between devices, shards(): lax.all_to_all(up_terms.astype(jnp.bfloat16), 'fsdp', split_axis=0, conca...  6.13 us
  transfers between devices with their start and end apart: 6, of which 4 were waited for; matrix products, arithmetic and copies ran while one was open for 8% of the time, Pallas kernels for 0%

profile of v1, /device:TPU:1, one launch (start us, length us, event | category | flops | bytes accessed | tf_op | source)
XLA Modules:
  0.0 300.3 jit_solution(17583600548639113353)
XLA Ops:
  8.1 0.8 convert_element_type.63
  8.9 0.9 convert_element_type.62
  9.8 0.6 pad_maximum_fusion
  10.4 1.0 copy.100
  11.4 0.8 fusion.10
  12.4 2.5 stack.2
  14.9 13.5 %all-to-all-start = ((bf16[64,128,256]{2,1,0:T(8,128)(2,1)}), bf16[64,128,256]{2,1,0:T(8,128)(2,1)}, u32[]{:S(2)}, u32[]{:S(2)}) async-start(bf16[64,128,256]{2,1,0:T(8,128)(2,1)} %stack.2), calls=%async_computation | async-start | bytes 8388608 | tf_op jit(solution)/shard_map/all_to_all | solution.py:134
  29.6 108.4 %all-to-all-done = bf16[64,128,256]{2,1,0:T(8,128)(2,1)} async-done(((bf16[64,128,256]{2,1,0:T(8,128)(2,1)}), bf16[64,128,256]{2,1,0:T(8,128)(2,1)}, u32[]{:S(2)}, u32[]{:S(2)}) %all-to-all-start) | async-done | bytes 4194336 | tf_op jit(solution)/shard_map/all_to_all | solution.py:134
  138.1 5.5 %convolution_convert_fusion = bf16[256,8192]{1,0:T(8,128)(2,1)} fusion(bf16[8192,256]{1,0:T(8,128)(2,1)} %bitcast.2, bf16[256,256]{1,0:T(8,128)(2,1)S(1)} %copy-done.2, pred[256]{0:T(512)(128)(4,1)S(1)} %broadcast_in_dim.105), kind=kOutput, calls=%fused_computation | convolution fusion | flops 1075904512 | bytes 8519936 | tf_op jit(solution)/shard_map/dot_general | solution.py:82
  143.6 1.1 split.9
  145.2 2.2 slice-done
  147.4 1.3 fusion.20
  149.7 0.7 broadcast_in_dim.127
  150.4 4.0 %all-to-all-start.1 = ((f32[4,1,8192]{2,1,0:T(1,128)}), f32[4,1,8192]{2,1,0:T(1,128)S(1)}, u32[]{:S(2)}, u32[]{:S(2)}) async-start(f32[4,1,8192]{2,1,0:T(1,128)} %broadcast_in_dim.127), calls=%async_computation.2 | async-start | bytes 262144 | tf_op jit(solution)/shard_map/all_to_all | solution.py:47
  154.5 7.0 %all-to-all-done.1 = f32[4,1,8192]{2,1,0:T(1,128)S(1)} async-done(((f32[4,1,8192]{2,1,0:T(1,128)}), f32[4,1,8192]{2,1,0:T(1,128)S(1)}, u32[]{:S(2)}, u32[]{:S(2)}) %all-to-all-start.1) | async-done | bytes 131104 | tf_op jit(solution)/shard_map/all_to_all | solution.py:47
  162.1 1.2 fusion.3
  163.3 6.1 %all-to-all-start.3 = ((bf16[64,16,256]{2,1,0:T(8,128)(2,1)}), bf16[64,16,256]{2,1,0:T(8,128)(2,1)S(1)}, u32[]{:S(2)}, u32[]{:S(2)}) async-start(bf16[64,16,256]{2,1,0:T(8,128)(2,1)} %bitcast.13), calls=%async_computation.4 | async-start | bytes 1048576 | tf_op jit(solution)/shard_map/all_to_all | solution.py:175
  169.4 3.2 %multiply_convert_fusion = bf16[1024,2048]{1,0:T(8,128)(2,1)} fusion(bf16[256,1024]{0,1:T(8,128)(2,1)S(1)} %bitcast.51, bf16[256,2048]{1,0:T(8,128)(2,1)S(1)} %copy-done), kind=kOutput, calls=%fused_computation.2 | convolution fusion | flops 1077936128 | bytes 5767168 | tf_op jit(solution)/shard_map/dot_general | solution.py:88
  172.6 14.1 %all-to-all-done.3 = bf16[64,16,256]{2,1,0:T(8,128)(2,1)S(1)} async-done(((bf16[64,16,256]{2,1,0:T(8,128)(2,1)}), bf16[64,16,256]{2,1,0:T(8,128)(2,1)S(1)}, u32[]{:S(2)}, u32[]{:S(2)}) %all-to-all-start.3) | async-done | bytes 524320 | tf_op jit(solution)/shard_map/all_to_all | solution.py:175
  186.7 6.6 %all-to-all-start.2 = ((bf16[64,16,2048]{2,1,0:T(8,128)(2,1)}), bf16[64,16,2048]{2,1,0:T(8,128)(2,1)}, u32[]{:S(2)}, u32[]{:S(2)}) async-start(bf16[64,16,2048]{2,1,0:T(8,128)(2,1)} %bitcast.49), calls=%async_computation.3 | async-start | bytes 8388608 | tf_op jit(solution)/shard_map/all_to_all | solution.py:172
  194.1 4.7 %fusion.2 = bf16[256,2048]{1,0:T(8,128)(2,1)} fusion(bf16[256,2048]{1,0:T(8,128)(2,1)} %reduce-scatter.2.cloned.1.call-done, bf16[256,16]{0,1:T(8,128)(2,1)S(1)} %copy.124, bf16[256,64]{0,1:T(8,128)(2,1)S(1)} %copy.117, bf16[64,16,2304]{2,1,0:T(8,128)(2,1)} %all-gather.2.cloned.1.call-done), kind=kOutput, calls=%fused_computation.6 | convolution fusion | flops 1076101120 | bytes 6332416 | tf_op jit(solution)/shard_map/dot_general | solution.py:162
  198.8 90.3 %all-to-all-done.2 = bf16[64,16,2048]{2,1,0:T(8,128)(2,1)} async-done(((bf16[64,16,2048]{2,1,0:T(8,128)(2,1)}), bf16[64,16,2048]{2,1,0:T(8,128)(2,1)}, u32[]{:S(2)}, u32[]{:S(2)}) %all-to-all-start.2) | async-done | bytes 4194336 | tf_op jit(solution)/shard_map/all_to_all | solution.py:172
  289.2 2.9 convert_reduce_fusion
  292.1 0.8 multiply_subtract_fusion
  (55 shorter events, 3.6 us)
Async XLA Ops:
  8.0 137.2 %copy-start = (bf16[256,2048]{1,0:T(8,128)(2,1)S(1)}, bf16[256,2048]{1,0:T(8,128)(2,1)}, u32[]{:S(2)}) copy-start(bf16[256,2048]{1,0:T(8,128)(2,1)} %param.13) | copy-start | bytes 3145732
  8.0 135.6 %all-gather.2.cloned.1.call-start = ((), (), s32[]{:S(2)}) async-start(), calls=%async_computation.6 | async-start | bytes 4792320 | tf_op jit(solution)/shard_map/all_gather | solution.py:42
  14.9 14.4 %copy-start.8 = (s32[64]{0:T(128)S(1)}, s32[64]{0:T(128)}, u32[]{:S(2)}) copy-start(s32[64]{0:T(128)} %param.19) | copy-start | bytes 772
  14.9 14.4 %copy-start.9 = (s32[16]{0:T(128)S(1)}, s32[16]{0:T(128)}, u32[]{:S(2)}) copy-start(s32[16]{0:T(128)} %param.17) | copy-start | bytes 196
  14.9 123.2 %copy-start.2 = (bf16[256,256]{1,0:T(8,128)(2,1)S(1)}, bf16[256,256]{1,0:T(8,128)(2,1)}, u32[]{:S(2)}) copy-start(bf16[256,256]{1,0:T(8,128)(2,1)} %param.14) | copy-start | bytes 393220
  14.9 123.2 %all-to-all-start = ((bf16[64,128,256]{2,1,0:T(8,128)(2,1)}), bf16[64,128,256]{2,1,0:T(8,128)(2,1)}, u32[]{:S(2)}, u32[]{:S(2)}) async-start(bf16[64,128,256]{2,1,0:T(8,128)(2,1)} %stack.2), calls=%async_computation | async-start | bytes 8388608 | tf_op jit(solution)/shard_map/all_to_all | solution.py:134
  28.4 165.7 %reduce-scatter.2.cloned.1.call-start = ((), (), s32[]{:S(2)}) async-start(), calls=%async_computation.5 | async-start | bytes 5242880 | tf_op jit(solution)/shard_map/reduce_scatter | solution.py:137
  145.2 2.2 slice-start
  150.4 11.1 %all-to-all-start.1 = ((f32[4,1,8192]{2,1,0:T(1,128)}), f32[4,1,8192]{2,1,0:T(1,128)S(1)}, u32[]{:S(2)}, u32[]{:S(2)}) async-start(f32[4,1,8192]{2,1,0:T(1,128)} %broadcast_in_dim.127), calls=%async_computation.2 | async-start | bytes 262144 | tf_op jit(solution)/shard_map/all_to_all | solution.py:47
  163.3 23.4 %all-to-all-start.3 = ((bf16[64,16,256]{2,1,0:T(8,128)(2,1)}), bf16[64,16,256]{2,1,0:T(8,128)(2,1)S(1)}, u32[]{:S(2)}, u32[]{:S(2)}) async-start(bf16[64,16,256]{2,1,0:T(8,128)(2,1)} %bitcast.13), calls=%async_computation.4 | async-start | bytes 1048576 | tf_op jit(solution)/shard_map/all_to_all | solution.py:175
  186.7 6.7 %copy-start.5 = (f32[1,16,256]{2,1,0:T(8,128)S(1)}, f32[1,16,256]{2,1,0:T(8,128)}, u32[]{:S(2)}) copy-start(f32[1,16,256]{2,1,0:T(8,128)} %param.21) | copy-start | bytes 49156
  186.7 6.7 %copy-start.6 = (f32[1,16,256]{2,1,0:T(8,128)S(1)}, f32[1,16,256]{2,1,0:T(8,128)}, u32[]{:S(2)}) copy-start(f32[1,16,256]{2,1,0:T(8,128)} %param.24) | copy-start | bytes 49156
  186.7 6.7 %copy-start.7 = (f32[1,16,256]{2,1,0:T(8,128)S(1)}, f32[1,16,256]{2,1,0:T(8,128)}, u32[]{:S(2)}) copy-start(f32[1,16,256]{2,1,0:T(8,128)} %param.25) | copy-start | bytes 49156
  186.7 102.5 %all-to-all-start.2 = ((bf16[64,16,2048]{2,1,0:T(8,128)(2,1)}), bf16[64,16,2048]{2,1,0:T(8,128)(2,1)}, u32[]{:S(2)}, u32[]{:S(2)}) async-start(bf16[64,16,2048]{2,1,0:T(8,128)(2,1)} %bitcast.49), calls=%async_computation.3 | async-start | bytes 8388608 | tf_op jit(solution)/shard_map/all_to_all | solution.py:172
  198.8 93.2 %copy-start.1 = (f32[1,16,2048]{2,1,0:T(8,128)S(1)}, f32[1,16,2048]{2,1,0:T(8,128)}, u32[]{:S(2)}) copy-start(f32[1,16,2048]{2,1,0:T(8,128)} %param.20) | copy-start | bytes 393220
  198.8 93.2 %copy-start.3 = (f32[1,16,2048]{2,1,0:T(8,128)S(1)}, f32[1,16,2048]{2,1,0:T(8,128)}, u32[]{:S(2)}) copy-start(f32[1,16,2048]{2,1,0:T(8,128)} %param.22) | copy-start | bytes 393220
  198.8 93.2 %copy-start.4 = (f32[1,16,2048]{2,1,0:T(8,128)S(1)}, f32[1,16,2048]{2,1,0:T(8,128)}, u32[]{:S(2)}) copy-start(f32[1,16,2048]{2,1,0:T(8,128)} %param.23) | copy-start | bytes 393220
Sparse Core Ops, SparseCore 0:
  12.1 105.0 all-gather.1
Sparse Core Ops, SparseCore 1:
  143.7 46.9 reduce-scatter.1
